TPU v7x, 32 devices: a whole 2x2x4 slice. The times are simulated.
32 devices in a mesh: wide: 8 (over z, x), narrow: 4 (over y, core).
Axes of the slice: x: 2, y: 2, z: 4, core: 2. Of those that a mesh axis runs over, the one named last changes fastest.
Arguments:
- embeddings: bfloat16 [16384, 1024], P(('wide', 'narrow')), may hold values from -32 to 32
- valid: int32 [16384], P(('wide', 'narrow')), may hold values from 0 to 1, as said below
Outputs:
- whitened: bfloat16 [16384, 1024], P(('wide', 'narrow'))
Inputs may be any that keep to these rules, and one draw needn't show every extreme that they name: The first row of every aligned block of 16 rows has valid = 1.
All inputs are finite; a program needn't handle non-finite values.
Results may differ from a plain program's by a relative error of at most 0.001.
Values sent between devices are 32-bit elements; how exact they have to be, the bound alone decides.
No kernel may reach another device: no remote copies, remote signals or barrier semaphores. Data moves between devices by JAX's collectives and lax.ppermute only.
A program may use at most 64 MiB of HBM per device.

v0:
```python
import jax
import jax.numpy as jnp
from jax import lax
from jax.sharding import PartitionSpec as P


def shifted_scatter(gram, count_local, sums_local, center):
    return (
        gram
        - sums_local[:, None] * center[None, :]
        - center[:, None] * sums_local[None, :]
        + count_local * center[:, None] * center[None, :]
    )


def narrow_rows(term):
    return lax.psum_scatter(term, "narrow", scatter_dimension=0, tiled=True)


def on_device(embeddings, valid):
    width = embeddings.shape[1]
    narrow_count = lax.axis_size("narrow")
    row_span = width // narrow_count
    offset = lax.axis_index("narrow") * row_span
    mask_half = valid.astype(jnp.bfloat16)
    count_local = jnp.sum(valid.astype(jnp.float32))
    masked = embeddings * mask_half[:, None]
    gram = lax.dot_general(
        masked, embeddings, (((0,), (0,)), ((), ())), preferred_element_type=jnp.float32
    )
    sums_local = jnp.dot(mask_half[None, :], embeddings, preferred_element_type=jnp.float32)[0]
    count, sums = lax.psum((count_local, sums_local), ("wide", "narrow"))
    term = shifted_scatter(gram, count_local, sums_local, sums / count)
    level_rows = narrow_rows(term)
    own_rows = lax.psum(level_rows, "wide")
    center = sums / count
    cov_rows = own_rows / count
    ident_rows = (
        lax.broadcasted_iota(jnp.int32, (row_span, width), 0) + offset
        == lax.broadcasted_iota(jnp.int32, (row_span, width), 1)
    ).astype(jnp.float32)
    diag_block = lax.dynamic_slice_in_dim(cov_rows, offset, row_span, 1)
    trace_part = jnp.sum(jnp.diagonal(diag_block))
    square_part = jnp.sum(cov_rows * cov_rows)
    trace_cov, square_sum = lax.psum((trace_part, square_part), "narrow")
    ridge_add = 0.05 * trace_cov / width + 1e-06
    norm_frob = jnp.sqrt(square_sum + 2.0 * ridge_add * trace_cov + width * ridge_add * ridge_add)
    base_rows = (cov_rows + ridge_add * ident_rows) / norm_frob
    root_rows = (3.0 * ident_rows - base_rows) / 2.0
    root_full = lax.all_gather(root_rows, "narrow", axis=0, tiled=True)
    first = jnp.dot(
        base_rows, root_full, precision=lax.Precision.HIGHEST, preferred_element_type=jnp.float32
    )
    second = jnp.dot(
        first, root_full, precision=lax.Precision.HIGHEST, preferred_element_type=jnp.float32
    )
    factor = (3.0 * ident_rows - second) / 2.0
    root_rows = jnp.dot(
        factor, root_full, precision=lax.Precision.HIGHEST, preferred_element_type=jnp.float32
    )
    centered_x = embeddings.astype(jnp.float32) - center
    product = jnp.dot(
        centered_x,
        lax.all_gather(root_rows, "narrow", axis=0, tiled=True),
        precision=lax.Precision.HIGHEST,
        preferred_element_type=jnp.float32,
    )
    return (product / jnp.sqrt(norm_frob)).astype(jnp.bfloat16)


def solution(mesh):
    in_specs = (P(("wide", "narrow"), None), P(("wide", "narrow")))
    out_specs = P(("wide", "narrow"), None)
    return jax.shard_map(
        on_device, mesh=mesh, in_specs=in_specs, out_specs=out_specs, check_vma=False
    )
```

profile of v0, /device:TPU:0, one launch (start us, length us, event | category | flops | bytes accessed | tf_op | source)
XLA Modules:
  0.0 300.6 jit_solution(4755402428084836865)
XLA Ops:
  6.5 0.0 reduce-scatter.2.cloned.1.call-start
  6.5 0.7 convert_element_type.14
  7.2 1.3 convert_reduce_fusion
  8.5 1.5 fusion.11
  10.0 42.1 %all-reduce = (f32[1024]{0:T(1024)S(1)}, f32[]{:T(128)}) all-reduce(f32[1024]{0:T(1024)S(1)} %bitcast.12, f32[]{:T(128)} %convert_reduce_fusion), channel_id=1, replica_groups=mesh['wide'=8,'narrow'=4] {'wide','narrow'}, use_global_device_ids=true, to_apply=%region_0.0 | all-reduce | flops 1025 | bytes 8200 | tf_op jit(solution)/shard_map/psum | solution.py:32
  52.1 1.3 broadcast_multiply_fusion
  53.4 5.3 %multiply_add_fusion = f32[1024,1024]{1,0:T(8,128)} fusion(bf16[512,1024]{1,0:T(8,128)(2,1)} %param.2, f32[1024]{0:T(1024)S(1)} %get-tuple-element.11, f32[1024]{0:T(1024)S(1)} %bitcast.13, f32[1024]{0:T(1024)S(1)} %get-tuple-element.12, bf16[512]{0:T(512)(128)(2,1)S(1)} %convert_element_type.14), kind=kOutput, calls=%fused_computation.1 | convolution fusion | flops 1080557568 | bytes 5256192 | tf_op jit(solution)/shard_map/dot_general | solution.py:28
  58.7 0.0 reduce-scatter.2.cloned.1.call-update
  58.7 0.0 all-reduce.4.cloned.1.call-start
  58.8 44.7 %reduce-scatter.2.cloned.1.call-done = f32[256,1024]{1,0:T(8,128)} async-done(((f32[1024,1024]{1,0:T(8,128)}), f32[256,1024]{1,0:T(8,128)}) %reduce-scatter.2.cloned.1.call-update) | async-done | bytes 1048592 | tf_op jit(solution)/shard_map/reduce_scatter | solution.py:17
  103.5 0.0 all-reduce.4.cloned.1.call-update
  103.5 0.0 all-gather.3.cloned.1.call-start
  103.6 81.6 %all-reduce.4.cloned.1.call-done = f32[256,1024]{1,0:T(8,128)} async-done(((f32[256,1024]{1,0:T(8,128)}), f32[256,1024]{1,0:T(8,128)}) %all-reduce.4.cloned.1.call-update) | async-done | bytes 1048592 | tf_op jit(solution)/shard_map/psum | solution.py:35
  185.2 2.7 multiply_reduce_fusion
  188.0 2.3 gather_fusion
  190.4 0.7 reduce_sum.28
  191.0 7.2 %all-reduce.1 = (f32[]{:T(128)}, f32[]{:T(128)}) all-reduce(f32[]{:T(128)} %get-tuple-element.9, f32[]{:T(128)} %reduce_sum.28), channel_id=1, replica_groups=mesh['wide'=8,'narrow'=4] {'narrow'}, use_global_device_ids=true, to_apply=%region_8.9 | all-reduce | flops 2 | bytes 16 | tf_op jit(solution)/shard_map/psum | solution.py:45
  200.3 1.3 fusion.7
  201.6 0.0 all-gather.3.cloned.1.call-update
  201.6 0.2 all-gather.5.cloned.1.call-start
  201.8 33.4 %all-gather.3.cloned.1.call-done = f32[1024,1024]{1,0:T(8,128)} async-done(((f32[256,1024]{1,0:T(8,128)}), f32[1024,1024]{1,0:T(8,128)}) %all-gather.3.cloned.1.call-update) | async-done | bytes 4194320 | tf_op jit(solution)/shard_map/all_gather | solution.py:50
  235.2 0.0 copy-start
  235.2 6.1 %fusion.10 = f32[256,1024]{1,0:T(8,128)S(1)} fusion(f32[1024,1024]{1,0:T(8,128)} %all-gather.3.cloned.1.call-done, f32[256,1024]{1,0:T(8,128)S(1)} %get-tuple-element.10, f32[]{:T(128)S(6)} %sqrt.6, f32[]{:T(128)S(6)} %add.45, s32[256]{0:T(256)S(1)} %iota_add_fusion), kind=kOutput, calls=%fused_computation.23 | convolution fusion | flops 3222274048 | bytes 6292488 | tf_op jit(solution)/shard_map/dot_general | solution.py:51
  241.4 0.0 copy-done
  241.4 3.7 %fusion.4 = f32[256,1024]{1,0:T(8,128)S(1)} fusion(f32[256,1024]{1,0:T(8,128)S(1)} %fusion.10, f32[1024,1024]{1,0:T(8,128)S(1)} %copy-done, s32[256]{0:T(256)S(1)} %iota_add_fusion), kind=kOutput, calls=%fused_computation.9 | convolution fusion | flops 3222274048 | bytes 6292480 | tf_op jit(solution)/shard_map/dot_general | solution.py:54
  245.1 0.0 copy-start.1
  245.2 4.7 %fusion.12 = f32[256,1024]{1,0:T(8,128)} fusion(f32[256,1024]{1,0:T(8,128)S(1)} %fusion.4, f32[1024,1024]{1,0:T(8,128)S(1)} %copy-done), kind=kOutput, calls=%fused_computation.25 | convolution fusion | flops 3221225472 | bytes 6291456 | tf_op jit(solution)/shard_map/dot_general | solution.py:58
  249.8 0.0 all-gather.5.cloned.1.call-update
  249.9 34.6 %all-gather.5.cloned.1.call-done = f32[1024,1024]{1,0:T(8,128)} async-done(((f32[256,1024]{1,0:T(8,128)}), f32[1024,1024]{1,0:T(8,128)}) %all-gather.5.cloned.1.call-update) | async-done | bytes 4194320 | tf_op jit(solution)/shard_map/all_gather | solution.py:64
  284.5 0.0 copy-done.1
  284.5 9.6 %divide_convert_fusion = bf16[512,1024]{1,0:T(8,128)(2,1)} fusion(f32[1024,1024]{1,0:T(8,128)} %all-gather.5.cloned.1.call-done, bf16[512,1024]{1,0:T(8,128)(2,1)S(1)} %copy-done.1, f32[]{:T(128)S(6)} %sqrt.7, f32[1024]{0:T(1024)S(1)} %get-tuple-element.12), kind=kOutput, calls=%fused_computation.2 | convolution fusion | flops 6444548096 | bytes 6295556 | tf_op jit(solution)/shard_map/dot_general | solution.py:62
  (4 shorter events, 0.0 us)
Async XLA Ops:
  6.5 97.0 %reduce-scatter.2.cloned.1.call-start = ((), (), s32[]{:S(2)}) async-start(), calls=%async_computation.1 | async-start | bytes 5242880 | tf_op jit(solution)/shard_map/reduce_scatter | solution.py:17
  58.7 126.5 %all-reduce.4.cloned.1.call-start = ((), (), s32[]{:S(2)}) async-start(), calls=%async_computation.2 | async-start | bytes 2097152 | tf_op jit(solution)/shard_map/psum | solution.py:35
  103.5 131.7 %all-gather.3.cloned.1.call-start = ((), (), s32[]{:S(2)}) async-start(), calls=%async_computation.3 | async-start | bytes 5242880 | tf_op jit(solution)/shard_map/all_gather | solution.py:50
  201.6 82.9 %all-gather.5.cloned.1.call-start = ((), (), s32[]{:S(2)}) async-start(), calls=%async_computation.4 | async-start | bytes 5242880 | tf_op jit(solution)/shard_map/all_gather | solution.py:64
  235.2 6.1 %copy-start = (f32[1024,1024]{1,0:T(8,128)S(1)}, f32[1024,1024]{1,0:T(8,128)}, u32[]{:S(2)}) copy-start(f32[1024,1024]{1,0:T(8,128)} %all-gather.3.cloned.1.call-done) | copy-start | bytes 12582916
  245.1 39.3 %copy-start.1 = (bf16[512,1024]{1,0:T(8,128)(2,1)S(1)}, bf16[512,1024]{1,0:T(8,128)(2,1)}, u32[]{:S(2)}) copy-start(bf16[512,1024]{1,0:T(8,128)(2,1)} %param.2) | copy-start | bytes 3145732
Sparse Core Ops, SparseCore 0:
  58.9 44.6 reduce-scatter.1
  107.0 78.1 all-reduce.3
  201.7 33.4 all-gather.2
  250.0 34.4 all-gather.4
where the time goes:
time: 301 us
  waiting for transfers between devices  194 us (64%)
  blocking collectives  49.3 us (16%)
  matrix products  30.9 us (10%)
  between operations  15.3 us (5%)
  other arithmetic  7.97 us (3%)
    psum x1, waiting for transfers between devices, on_device(): own_rows = lax.psum(level_rows, 'wide')  81.6 us
    reduce_scatter x1, waiting for transfers between devices, narrow_rows(): return lax.psum_scatter(term, 'narrow', scatter_dimension=0, tiled=True)  44.7 us
    psum x1, blocking collectives, on_device(): count, sums = lax.psum((count_local, sums_local), ('wide', 'narrow'))  42.1 us
    all_gather x1, waiting for transfers between devices, on_device(): lax.all_gather(root_rows, 'narrow', axis=0, tiled=True)  34.6 us
    all_gather x1, waiting for transfers between devices, on_device(): root_full = lax.all_gather(root_rows, 'narrow', axis=0, tiled=True)  33.4 us
    dot_general x1, matrix products, on_device(): jnp.dot(centered_x, lax.all_gather(root_rows, 'narrow', axis=0, tiled=Tru...  9.62 us
    psum x1, blocking collectives, on_device(): trace_cov, square_sum = lax.psum((trace_part, square_part), 'narrow')  7.19 us
    dot_general x1, matrix products, on_device(): jnp.dot(base_rows, root_full, precision=lax.Precision.HIGHEST, preferred_...  6.13 us
  transfers between devices with their start and end apart: 4, of which 4 were waited for; matrix products, arithmetic and copies ran while one was open for 0% of the time, Pallas kernels for 0%

commit v1 on v0

--- a/solution.py
+++ b/solution.py
@@ -32,7 +32,9 @@
     count, sums = lax.psum((count_local, sums_local), ("wide", "narrow"))
     term = shifted_scatter(gram, count_local, sums_local, sums / count)
     level_rows = narrow_rows(term)
-    own_rows = lax.psum(level_rows, "wide")
+    own_rows = level_rows
+    for hop in (1, 2, 4):
+        own_rows = own_rows + lax.ppermute(own_rows, "wide", [(dev, dev ^ hop) for dev in range(8)])
     center = sums / count
     cov_rows = own_rows / count
     ident_rows = (

time: 301 us -> 316 us (1.050)
  waiting for transfers between devices: 194 us -> 205 us
  starting transfers between devices: 0.3 us -> 5.72 us
    ppermute x0 -> x3, waiting for transfers between devices: none -> 89.9 us  [on_device(): lax.ppermute(own_rows, 'wide', [(dev, dev ^ hop) for dev in range(8)])]
    psum x1 -> x0, waiting for transfers between devices: 81.6 us -> none  [on_device(): own_rows = lax.psum(level_rows, 'wide')]
    ppermute x0 -> x3, starting transfers between devices: none -> 5.46 us  [on_device(): lax.ppermute(own_rows, 'wide', [(dev, dev ^ hop) for dev in range(8)])]
  transfers between devices with their start and end apart: 4 -> 6, of which waited for: 4 -> 6; matrix products, arithmetic and copies ran while one was open for 0% -> 0% of each run, Pallas kernels for 0% -> 0%
where the time goes in v1:
time: 316 us
  waiting for transfers between devices  205 us (65%)
  blocking collectives  48.4 us (15%)
  matrix products  31 us (10%)
  between operations  15 us (5%)
  other arithmetic  8.36 us (3%)
  starting transfers between devices  5.72 us (2%)
    ppermute x3, waiting for transfers between devices, on_device(): lax.ppermute(own_rows, 'wide', [(dev, dev ^ hop) for dev in range(8)])  89.9 us
    reduce_scatter x1, waiting for transfers between devices, narrow_rows(): return lax.psum_scatter(term, 'narrow', scatter_dimension=0, tiled=True)  44.8 us
    psum x1, blocking collectives, on_device(): count, sums = lax.psum((count_local, sums_local), ('wide', 'narrow'))  42.1 us
    all_gather x1, waiting for transfers between devices, on_device(): root_full = lax.all_gather(root_rows, 'narrow', axis=0, tiled=True)  35.5 us
    all_gather x1, waiting for transfers between devices, on_device(): lax.all_gather(root_rows, 'narrow', axis=0, tiled=True)  34.6 us
    dot_general x1, matrix products, on_device(): jnp.dot(centered_x, lax.all_gather(root_rows, 'narrow', axis=0, tiled=Tru...  9.62 us
  transfers between devices with their start and end apart: 6, of which 6 were waited for; matrix products, arithmetic and copies ran while one was open for 0% of the time, Pallas kernels for 0%

profile of v1, /device:TPU:0, one launch (start us, length us, event | category | flops | bytes accessed | tf_op | source)
XLA Modules:
  0.0 315.6 jit_solution(11353250062281078673)
XLA Ops:
  6.5 0.0 reduce-scatter.2.cloned.1.call-start
  6.5 0.7 convert_element_type.14
  7.2 1.3 convert_reduce_fusion
  8.5 1.5 fusion.11
  10.0 42.1 %all-reduce = (f32[1024]{0:T(1024)S(1)}, f32[]{:T(128)}) all-reduce(f32[1024]{0:T(1024)S(1)} %bitcast.12, f32[]{:T(128)} %convert_reduce_fusion), channel_id=1, replica_groups=mesh['wide'=8,'narrow'=4] {'wide','narrow'}, use_global_device_ids=true, to_apply=%region_0.0 | all-reduce | flops 1025 | bytes 8200 | tf_op jit(solution)/shard_map/psum | solution.py:32
  52.1 1.3 broadcast_multiply_fusion
  53.4 5.3 %multiply_add_fusion = f32[1024,1024]{1,0:T(8,128)} fusion(bf16[512,1024]{1,0:T(8,128)(2,1)} %param.2, f32[1024]{0:T(1024)S(1)} %get-tuple-element.11, f32[1024]{0:T(1024)S(1)} %bitcast.13, f32[1024]{0:T(1024)S(1)} %get-tuple-element.12, bf16[512]{0:T(512)(128)(2,1)S(1)} %convert_element_type.14), kind=kOutput, calls=%fused_computation.1 | convolution fusion | flops 1080557568 | bytes 5256192 | tf_op jit(solution)/shard_map/dot_general | solution.py:28
  58.7 0.0 reduce-scatter.2.cloned.1.call-update
  58.7 0.0 all-gather.3.cloned.1.call-start
  58.8 44.8 %reduce-scatter.2.cloned.1.call-done = f32[256,1024]{1,0:T(8,128)} async-done(((f32[1024,1024]{1,0:T(8,128)}), f32[256,1024]{1,0:T(8,128)}) %reduce-scatter.2.cloned.1.call-update) | async-done | bytes 1048592 | tf_op jit(solution)/shard_map/reduce_scatter | solution.py:17
  103.6 1.5 collective-permute-start
  105.0 23.5 %collective-permute-done = f32[256,1024]{1,0:T(8,128)S(1)} collective-permute-done((f32[256,1024]{1,0:T(8,128)}, f32[256,1024]{1,0:T(8,128)S(1)}, u32[]{:S(2)}, u32[]{:S(2)}) %collective-permute-start) | collective-permute-done | bytes 1048608 | tf_op jit(solution)/shard_map/ppermute | solution.py:37
  128.5 1.4 add.51
  129.9 1.5 collective-permute-start.1
  131.5 22.4 %collective-permute-done.1 = f32[256,1024]{1,0:T(8,128)S(1)} collective-permute-done((f32[256,1024]{1,0:T(8,128)S(1)}, f32[256,1024]{1,0:T(8,128)S(1)}, u32[]{:S(2)}, u32[]{:S(2)}) %collective-permute-start.1) | collective-permute-done | bytes 1048608 | tf_op jit(solution)/shard_map/ppermute | solution.py:37
  153.9 0.2 add.52
  154.1 2.5 collective-permute-start.2
  156.5 44.0 %collective-permute-done.2 = f32[256,1024]{1,0:T(8,128)S(1)} collective-permute-done((f32[256,1024]{1,0:T(8,128)S(1)}, f32[256,1024]{1,0:T(8,128)S(1)}, u32[]{:S(2)}, u32[]{:S(2)}) %collective-permute-start.2) | collective-permute-done | bytes 1048608 | tf_op jit(solution)/shard_map/ppermute | solution.py:37
  200.6 1.6 multiply_reduce_fusion
  202.2 2.3 gather_fusion
  204.6 0.6 reduce_sum.28
  205.1 6.3 %all-reduce.1 = (f32[]{:T(128)}, f32[]{:T(128)}) all-reduce(f32[]{:T(128)} %get-tuple-element.9, f32[]{:T(128)} %reduce_sum.28), channel_id=1, replica_groups=mesh['wide'=8,'narrow'=4] {'narrow'}, use_global_device_ids=true, to_apply=%region_7.8 | all-reduce | flops 2 | bytes 16 | tf_op jit(solution)/shard_map/psum | solution.py:47
  213.2 1.3 fusion.7
  214.5 0.0 all-gather.3.cloned.1.call-update
  214.5 0.2 all-gather.5.cloned.1.call-start
  214.8 35.5 %all-gather.3.cloned.1.call-done = f32[1024,1024]{1,0:T(8,128)} async-done(((f32[256,1024]{1,0:T(8,128)}), f32[1024,1024]{1,0:T(8,128)}) %all-gather.3.cloned.1.call-update) | async-done | bytes 4194320 | tf_op jit(solution)/shard_map/all_gather | solution.py:52
  250.2 0.0 copy-start
  250.2 6.1 %fusion.10 = f32[256,1024]{1,0:T(8,128)S(1)} fusion(f32[1024,1024]{1,0:T(8,128)} %all-gather.3.cloned.1.call-done, f32[256,1024]{1,0:T(8,128)S(1)} %get-tuple-element.10, f32[]{:T(128)S(6)} %sqrt.6, f32[]{:T(128)S(6)} %add.55, s32[256]{0:T(256)S(1)} %iota_add_fusion), kind=kOutput, calls=%fused_computation.23 | convolution fusion | flops 3222274048 | bytes 6292488 | tf_op jit(solution)/shard_map/dot_general | solution.py:53
  256.4 0.0 copy-done
  256.4 3.7 %fusion.4 = f32[256,1024]{1,0:T(8,128)S(1)} fusion(f32[256,1024]{1,0:T(8,128)S(1)} %fusion.10, f32[1024,1024]{1,0:T(8,128)S(1)} %copy-done, s32[256]{0:T(256)S(1)} %iota_add_fusion), kind=kOutput, calls=%fused_computation.9 | convolution fusion | flops 3222274048 | bytes 6292480 | tf_op jit(solution)/shard_map/dot_general | solution.py:56
  260.1 0.0 copy-start.1
  260.1 4.7 %fusion.12 = f32[256,1024]{1,0:T(8,128)} fusion(f32[256,1024]{1,0:T(8,128)S(1)} %fusion.4, f32[1024,1024]{1,0:T(8,128)S(1)} %copy-done), kind=kOutput, calls=%fused_computation.25 | convolution fusion | flops 3221225472 | bytes 6291456 | tf_op jit(solution)/shard_map/dot_general | solution.py:60
  264.8 0.0 all-gather.5.cloned.1.call-update
  264.9 34.6 %all-gather.5.cloned.1.call-done = f32[1024,1024]{1,0:T(8,128)} async-done(((f32[256,1024]{1,0:T(8,128)}), f32[1024,1024]{1,0:T(8,128)}) %all-gather.5.cloned.1.call-update) | async-done | bytes 4194320 | tf_op jit(solution)/shard_map/all_gather | solution.py:66
  299.5 0.0 copy-done.1
  299.5 9.6 %divide_convert_fusion = bf16[512,1024]{1,0:T(8,128)(2,1)} fusion(f32[1024,1024]{1,0:T(8,128)} %all-gather.5.cloned.1.call-done, bf16[512,1024]{1,0:T(8,128)(2,1)S(1)} %copy-done.1, f32[]{:T(128)S(6)} %sqrt.7, f32[1024]{0:T(1024)S(1)} %get-tuple-element.12), kind=kOutput, calls=%fused_computation.2 | convolution fusion | flops 6444548096 | bytes 6295556 | tf_op jit(solution)/shard_map/dot_general | solution.py:64
  (4 shorter events, 0.0 us)
Async XLA Ops:
  6.5 97.0 %reduce-scatter.2.cloned.1.call-start = ((), (), s32[]{:S(2)}) async-start(), calls=%async_computation.1 | async-start | bytes 5242880 | tf_op jit(solution)/shard_map/reduce_scatter | solution.py:17
  58.7 191.5 %all-gather.3.cloned.1.call-start = ((), (), s32[]{:S(2)}) async-start(), calls=%async_computation.2 | async-start | bytes 5242880 | tf_op jit(solution)/shard_map/all_gather | solution.py:52
  103.6 25.0 %collective-permute-start = (f32[256,1024]{1,0:T(8,128)}, f32[256,1024]{1,0:T(8,128)S(1)}, u32[]{:S(2)}, u32[]{:S(2)}) collective-permute-start(f32[256,1024]{1,0:T(8,128)} %reduce-scatter.2.cloned.1.call-done), channel_id=1, source_target_pairs={{0,4},{4,0},{8,12},{12,8},{16,20},{20,16},{24,28},{28,24},{1,5},{5... | collective-permute-start | bytes 3145736 | tf_op jit(solution)/shard_map/ppermute | solution.py:37
  129.9 24.0 %collective-permute-start.1 = (f32[256,1024]{1,0:T(8,128)S(1)}, f32[256,1024]{1,0:T(8,128)S(1)}, u32[]{:S(2)}, u32[]{:S(2)}) collective-permute-start(f32[256,1024]{1,0:T(8,128)S(1)} %add.51), channel_id=1, source_target_pairs={{0,8},{4,12},{8,0},{12,4},{16,24},{20,28},{24,16},{28,20},{1,9},{5... | collective-permute-start | bytes 3145736 | tf_op jit(solution)/shard_map/ppermute | solution.py:37
  154.1 46.5 %collective-permute-start.2 = (f32[256,1024]{1,0:T(8,128)S(1)}, f32[256,1024]{1,0:T(8,128)S(1)}, u32[]{:S(2)}, u32[]{:S(2)}) collective-permute-start(f32[256,1024]{1,0:T(8,128)S(1)} %add.52), channel_id=1, source_target_pairs={{0,16},{4,20},{8,24},{12,28},{16,0},{20,4},{24,8},{28,12},{1,17},{... | collective-permute-start | bytes 3145736 | tf_op jit(solution)/shard_map/ppermute | solution.py:37
  214.5 84.9 %all-gather.5.cloned.1.call-start = ((), (), s32[]{:S(2)}) async-start(), calls=%async_computation.3 | async-start | bytes 5242880 | tf_op jit(solution)/shard_map/all_gather | solution.py:66
  250.2 6.1 %copy-start = (f32[1024,1024]{1,0:T(8,128)S(1)}, f32[1024,1024]{1,0:T(8,128)}, u32[]{:S(2)}) copy-start(f32[1024,1024]{1,0:T(8,128)} %all-gather.3.cloned.1.call-done) | copy-start | bytes 12582916
  260.1 39.3 %copy-start.1 = (bf16[512,1024]{1,0:T(8,128)(2,1)S(1)}, bf16[512,1024]{1,0:T(8,128)(2,1)}, u32[]{:S(2)}) copy-start(bf16[512,1024]{1,0:T(8,128)(2,1)} %param.2) | copy-start | bytes 3145732
Sparse Core Ops, SparseCore 0:
  58.9 44.6 reduce-scatter.1
  214.7 35.5 all-gather.2
  265.0 34.4 all-gather.4
